TPU v7x, 256 devices: a whole 4x4x8 slice. The times are simulated.
256 devices in a mesh: dp: 32 (over y, x, core), tensor: 8 (over z).
Axes of the slice: x: 4, y: 4, z: 8, core: 2. Of those that a mesh axis runs over, the one named last changes fastest.
Arguments:
- hidden: bfloat16 [32, 1024, 4096], P('dp', None, 'tensor'), as said below
- gain: float32 [4096], replicated, may hold values from 0.5 to 1.5
- head: bfloat16 [4096, 131072], P(None, ('dp', 'tensor'))
- lengths: int32 [32], P('dp'), may hold values from 256 to 1024, as said below
- offsets: int32 [32, 32], P('dp'), may hold values from 0 to 255
- targets: int32 [32, 32], P('dp'), may hold values from 0 to 131071
- mask: int32 [32, 32], P('dp'), may hold values from 0 to 1, as said below
Outputs:
- logprob: float32 [32, 32], P('dp')
- entropy: float32 [32, 32], P('dp')
Inputs may be any that keep to these rules, and one draw needn't show every extreme that they name: `lengths`: each length is at least 256; some sequence has length exactly 1024 in every draw. `mask`: among the 32 slots of the sequences of one index of dp, at most 16 are scored; some index of dp has exactly 16. `hidden`: entries are of order one or a few tens in magnitude.
All inputs are finite; a program needn't handle non-finite values.
Results may differ from a plain program's by a relative error of at most 0.0089.
Values may be sent and summed in bfloat16 or wider, within the bound.
A program may use at most 64 MiB of HBM per device.

v0:
```python
import jax
import jax.numpy as jnp
from jax import lax
from jax.sharding import PartitionSpec as P


def per_device(hidden, gain, head, lengths, offsets, targets, mask):
    seq_count, slot_count = offsets.shape
    local_rows = seq_count * slot_count
    position = lengths[:, None] - 1 - offsets
    picked = jnp.take_along_axis(hidden, position[:, :, None], axis=1)
    picked = picked.reshape(local_rows, hidden.shape[2])
    full_rows = lax.all_gather(picked, "tensor", axis=1, tiled=True)
    values = full_rows.astype(jnp.float32)
    meansq = jnp.mean(values * values, axis=-1, keepdims=True)
    normed = (values * lax.rsqrt(meansq + 1e-06) * gain).astype(jnp.bfloat16)
    flat_target = targets.reshape(local_rows)
    flat_mask = mask.reshape(local_rows)
    block_rows = normed.shape[0]
    vocab_width = head.shape[1]
    vocab_start = (
        lax.axis_index("dp") * lax.axis_size("tensor") + lax.axis_index("tensor")
    ) * vocab_width
    columns = jnp.arange(vocab_width, dtype=jnp.int32)
    rows_piece = lax.all_gather(normed, "dp", axis=0, tiled=True)
    target_piece = lax.all_gather(flat_target, "dp", axis=0, tiled=True)
    logits = jnp.dot(rows_piece, head, preferred_element_type=jnp.float32)
    top = jnp.max(logits, axis=-1)
    expo = jnp.exp(logits - top[:, None])
    total = jnp.sum(expo, axis=-1)
    weighted = jnp.sum(expo * logits, axis=-1)
    hit = columns[None, :] == (target_piece - vocab_start)[:, None]
    chosen = jnp.sum(jnp.where(hit, logits, 0.0), axis=-1)
    fresh = (top, total, weighted, chosen)
    stats = tuple((new for new in fresh))
    top = lax.pmax(stats[0], ("dp", "tensor"))
    factor = jnp.exp(stats[0] - top)
    total, weighted, chosen = lax.psum(
        (stats[1] * factor, stats[2] * factor, stats[3]), ("dp", "tensor")
    )
    lse = top + jnp.log(total)
    score = chosen - lse
    spread = lse - weighted / total
    offset_rows = lax.axis_index("dp") * block_rows
    score = lax.dynamic_slice_in_dim(score, offset_rows, block_rows)
    spread = lax.dynamic_slice_in_dim(spread, offset_rows, block_rows)
    keep = flat_mask.astype(jnp.float32)
    logprob = (keep * score).reshape(seq_count, slot_count)
    entropy = (keep * spread).reshape(seq_count, slot_count)
    return (logprob, entropy)


def solution(mesh):
    return jax.shard_map(
        per_device,
        mesh=mesh,
        in_specs=(
            P("dp", None, "tensor"),
            P(),
            P(None, ("dp", "tensor")),
            P("dp"),
            P("dp", None),
            P("dp", None),
            P("dp", None),
        ),
        out_specs=(P("dp", None), P("dp", None)),
        check_vma=False,
    )
```

profile of v0, /device:TPU:1, one launch (start us, length us, event | category | flops | bytes accessed | tf_op | source)
XLA Modules:
  0.0 265.7 jit_solution(5815184149624589043)
XLA Ops:
  7.2 0.0 copy-start
  7.2 0.0 all-gather.3.cloned.1.call-start
  7.9 0.7 fusion.7
  8.6 0.7 compare_and_fusion
  9.3 0.0 copy-done
  9.3 0.6 gather_fusion
  9.9 0.1 broadcast_select_fusion
  10.0 23.3 %all_gather.10 = bf16[32,4096]{1,0:T(8,128)(2,1)S(1)} all-gather(bf16[32,512]{1,0:T(8,128)(2,1)S(1)} %broadcast_select_fusion), channel_id=1, replica_groups=mesh['dp'=32,'tensor'=8] {'tensor'}, dimensions={1}, use_global_device_ids=true | all-gather | bytes 294912 | tf_op jit(solution)/shard_map/all_gather | solution.py:13
  33.3 0.2 fusion.1
  33.4 1.6 fusion.3
  35.0 0.0 all-gather.3.cloned.1.call-update
  35.0 1.3 dynamic-slice
  37.0 0.8 bitcast_dynamic-update-slice_fusion
  37.7 19.8 %all-reduce = s32[1024]{0:T(1024)S(1)} all-reduce(s32[1024]{0:T(1024)S(1)} %bitcast_dynamic-update-slice_fusion), channel_id=2, replica_groups=mesh['dp'=32,'tensor'=8] {'dp'}, use_global_device_ids=true, to_apply=%add | all-reduce | flops 1024 | bytes 8192
  57.6 41.2 %all-gather.3.cloned.1.call-done = bf16[1024,4096]{1,0:T(8,128)(2,1)} async-done(((bf16[32,4096]{1,0:T(8,128)(2,1)}), bf16[1024,4096]{1,0:T(8,128)(2,1)}) %all-gather.3.cloned.1.call-update) | async-done | bytes 8388624 | tf_op jit(solution)/shard_map/all_gather | solution.py:25
  98.8 8.3 %fusion.10 = (f32[1024]{0:T(1024)S(1)}, f32[1024,512]{0,1:T(8,128)S(1)}) fusion(bf16[1024,4096]{1,0:T(8,128)(2,1)} %all-gather.3.cloned.1.call-done, bf16[4096,512]{1,0:T(8,128)(2,1)} %param.9), kind=kOutput, calls=%fused_computation.30 | convolution fusion | flops 4295490560 | bytes 14684160 | tf_op jit(solution)/shard_map/dot_general | solution.py:27
  107.1 0.0 copy-start.1
  107.1 75.8 %pmax.7 = f32[1024]{0:T(1024)S(1)} all-reduce(f32[1024]{0:T(1024)S(1)} %get-tuple-element.14), channel_id=1, replica_groups=mesh['dp'=32,'tensor'=8] {'dp','tensor'}, use_global_device_ids=true, to_apply=%region_4.5 | all-reduce | flops 1024 | bytes 8192 | tf_op jit(solution)/shard_map/pmax | solution.py:36
  182.9 0.7 multiply_reduce_fusion
  183.6 74.6 %all-reduce.1 = (f32[1024]{0:T(1024)S(1)}, f32[1024]{0:T(1024)S(1)}, f32[1024]{0:T(1024)S(1)}) all-reduce(f32[1024]{0:T(1024)S(1)} %get-tuple-element.4, f32[1024]{0:T(1024)S(1)} %get-tuple-element.11, f32[1024]{0:T(1024)S(1)} %get-tuple-element.10), channel_id=1, replica_groups=mesh['dp'=32,'tensor'=8] {'dp','tensor'}, use_global_device_ids=true, to_apply=%region_2.3 | all-reduce | flops 3072 | bytes 24576 | tf_op jit(solution)/shard_map/psum | solution.py:38
  258.3 0.0 copy-done.1
  258.3 0.6 fusion.9
  (6 shorter events, 0.0 us)
Async XLA Ops:
  7.2 2.1 copy-start
  7.2 91.7 %all-gather.3.cloned.1.call-start = ((), (), s32[]{:S(2)}) async-start(), calls=%async_computation | async-start | bytes 8650752 | tf_op jit(solution)/shard_map/all_gather | solution.py:25
  107.1 151.1 %copy-start.1 = (s32[1,32]{1,0:T(1,128)S(1)}, s32[1,32]{1,0:T(1,128)}, u32[]{:S(2)}) copy-start(s32[1,32]{1,0:T(1,128)} %param.13) | copy-start | bytes 388
Sparse Core Ops, SparseCore 0:
  35.2 63.6 all-gather.2
where the time goes:
time: 266 us
  blocking collectives  194 us (73%)
  waiting for transfers between devices  41.3 us (16%)
  between operations  15.5 us (6%)
  matrix products  8.27 us (3%)
  other arithmetic  4.44 us (2%)
  local copies, waits for them, and re-layouts  2.68 us (1%)
    pmax x1, blocking collectives, per_device(): top = lax.pmax(stats[0], ('dp', 'tensor'))  75.8 us
    psum x1, blocking collectives, per_device(): lax.psum((stats[1] * factor, stats[2] * factor, stats[3]), ('dp', 'tensor'))  74.6 us
    all_gather x1, waiting for transfers between devices, per_device(): rows_piece = lax.all_gather(normed, 'dp', axis=0, tiled=True)  41.2 us
    all_gather x1, blocking collectives, per_device(): full_rows = lax.all_gather(picked, 'tensor', axis=1, tiled=True)  23.3 us
    unnamed x1, blocking collectives  19.8 us
    dot_general x1, matrix products, per_device(): logits = jnp.dot(rows_piece, head, preferred_element_type=jnp.float32)  8.27 us
  transfers between devices with their start and end apart: 1, of which 1 were waited for; matrix products, arithmetic and copies ran while one was open for 1% of the time, Pallas kernels for 0%

commit v1 on v0

--- a/solution.py
+++ b/solution.py
@@ -22,7 +22,9 @@
         lax.axis_index("dp") * lax.axis_size("tensor") + lax.axis_index("tensor")
     ) * vocab_width
     columns = jnp.arange(vocab_width, dtype=jnp.int32)
-    rows_piece = lax.all_gather(normed, "dp", axis=0, tiled=True)
+    rows_piece = jnp.concatenate(
+        lax.all_to_all(jnp.stack([normed] * lax.axis_size("dp")), "dp", 0, 0), axis=0
+    )
     target_piece = lax.all_gather(flat_target, "dp", axis=0, tiled=True)
     logits = jnp.dot(rows_piece, head, preferred_element_type=jnp.float32)
     top = jnp.max(logits, axis=-1)

time: 266 us -> 315 us (1.18)
  blocking collectives: 194 us -> 281 us
  waiting for transfers between devices: 41.3 us -> 0.01 us
  starting transfers between devices: 0.04 us -> 14.1 us
  between operations: 15.5 us -> 2.11 us
    unnamed x1, blocking collectives: 19.8 us -> 108 us
    all_gather x1 -> x0, waiting for transfers between devices: 41.2 us -> none  [per_device(): rows_piece = lax.all_gather(normed, 'dp', axis=0, tiled=True)]
    all_to_all x0 -> x1, starting transfers between devices: none -> 14.1 us  [per_device(): lax.all_to_all(jnp.stack([normed] * lax.axis_size('dp')), 'dp', 0, 0)]
    another operation x0 -> x1, local copies, waits for them, and re-layouts: none -> 4.26 us  [per_device(): jnp.stack([normed] * lax.axis_size('dp'))]
  transfers between devices with their start and end apart: 1 -> 1, of which waited for: 1 -> 0; matrix products, arithmetic and copies ran while one was open for 1% -> 0% of each run, Pallas kernels for 0% -> 0%
where the time goes in v1:
time: 315 us
  blocking collectives  281 us (89%)
  starting transfers between devices  14.1 us (4%)
  matrix products  8.28 us (3%)
  local copies, waits for them, and re-layouts  5.61 us (2%)
  other arithmetic  3.73 us (1%)
    unnamed x1, blocking collectives  108 us
    pmax x1, blocking collectives, per_device(): top = lax.pmax(stats[0], ('dp', 'tensor'))  77.1 us
    psum x1, blocking collectives, per_device(): lax.psum((stats[1] * factor, stats[2] * factor, stats[3]), ('dp', 'tensor'))  72.7 us
    all_gather x1, blocking collectives, per_device(): full_rows = lax.all_gather(picked, 'tensor', axis=1, tiled=True)  23.3 us
    all_to_all x1, starting transfers between devices, per_device(): lax.all_to_all(jnp.stack([normed] * lax.axis_size('dp')), 'dp', 0, 0)  14.1 us
    dot_general x1, matrix products, per_device(): logits = jnp.dot(rows_piece, head, preferred_element_type=jnp.float32)  8.28 us
  transfers between devices with their start and end apart: 1, of which 0 were waited for; matrix products, arithmetic and copies ran while one was open for 0% of the time, Pallas kernels for 0%

profile of v1, /device:TPU:1, one launch (start us, length us, event | category | flops | bytes accessed | tf_op | source)
XLA Modules:
  0.0 314.5 jit_solution(6621209808135955841)
XLA Ops:
  0.6 0.0 copy-start
  1.4 0.7 fusion.7
  2.0 0.7 compare_and_fusion
  2.7 0.0 copy-done
  2.7 0.6 gather_fusion
  3.4 0.1 broadcast_select_fusion
  3.4 23.3 %all_gather.7 = bf16[32,4096]{1,0:T(8,128)(2,1)S(1)} all-gather(bf16[32,512]{1,0:T(8,128)(2,1)S(1)} %broadcast_select_fusion), channel_id=1, replica_groups=mesh['dp'=32,'tensor'=8] {'tensor'}, dimensions={1}, use_global_device_ids=true | all-gather | bytes 294912 | tf_op jit(solution)/shard_map/all_gather | solution.py:13
  26.7 0.2 fusion.1
  26.9 0.9 fusion.3
  27.7 4.3 %stack.2 = bf16[32,32,4096]{2,1,0:T(8,128)(2,1)} broadcast(bf16[32,4096]{1,0:T(8,128)(2,1)S(1)} %fusion.3), dimensions={1,2} | broadcast | bytes 8650752 | tf_op jit(solution)/shard_map/stack | solution.py:26
  32.0 0.0 copy-start.3
  32.0 0.0 copy-start.2
  32.0 14.1 %all-to-all-start = ((bf16[32,32,4096]{2,1,0:T(8,128)(2,1)}), bf16[32,32,4096]{2,1,0:T(8,128)(2,1)}, u32[]{:S(2)}, u32[]{:S(2)}) async-start(bf16[32,32,4096]{2,1,0:T(8,128)(2,1)} %stack.2), calls=%async_computation | async-start | bytes 16777216 | tf_op jit(solution)/shard_map/all_to_all | solution.py:26
  46.1 0.0 copy-done.3
  46.1 0.6 dynamic-slice
  47.3 0.0 copy-done.2
  47.3 0.1 bitcast_dynamic-update-slice_fusion
  47.5 107.7 %all-reduce = s32[1024]{0:T(1024)S(1)} all-reduce(s32[1024]{0:T(1024)S(1)} %bitcast_dynamic-update-slice_fusion), channel_id=2, replica_groups=mesh['dp'=32,'tensor'=8] {'dp'}, use_global_device_ids=true, to_apply=%add | all-reduce | flops 1024 | bytes 8192
  155.1 0.0 all-to-all-done
  155.1 8.3 %fusion.10 = (f32[1024]{0:T(1024)S(1)}, f32[1024,512]{0,1:T(8,128)S(1)}) fusion(bf16[1024,4096]{1,0:T(8,128)(2,1)} %bitcast.8, bf16[4096,512]{1,0:T(8,128)(2,1)} %param.9), kind=kOutput, calls=%fused_computation.30 | convolution fusion | flops 4295490560 | bytes 14684160 | tf_op jit(solution)/shard_map/dot_general | solution.py:29
  163.4 0.0 copy-start.1
  163.4 77.1 %pmax.7 = f32[1024]{0:T(1024)S(1)} all-reduce(f32[1024]{0:T(1024)S(1)} %get-tuple-element.14), channel_id=1, replica_groups=mesh['dp'=32,'tensor'=8] {'dp','tensor'}, use_global_device_ids=true, to_apply=%region_4.5 | all-reduce | flops 1024 | bytes 8192 | tf_op jit(solution)/shard_map/pmax | solution.py:38
  240.5 0.7 multiply_reduce_fusion
  241.2 72.7 %all-reduce.1 = (f32[1024]{0:T(1024)S(1)}, f32[1024]{0:T(1024)S(1)}, f32[1024]{0:T(1024)S(1)}) all-reduce(f32[1024]{0:T(1024)S(1)} %get-tuple-element.4, f32[1024]{0:T(1024)S(1)} %get-tuple-element.11, f32[1024]{0:T(1024)S(1)} %get-tuple-element.10), channel_id=1, replica_groups=mesh['dp'=32,'tensor'=8] {'dp','tensor'}, use_global_device_ids=true, to_apply=%region_2.3 | all-reduce | flops 3072 | bytes 24576 | tf_op jit(solution)/shard_map/psum | solution.py:40
  313.9 0.0 copy-done.1
  313.9 0.6 fusion.9
  (6 shorter events, 0.0 us)
Async XLA Ops:
  0.6 2.1 copy-start
  32.0 14.1 %copy-start.3 = (u32[256]{0:T(256)S(1)}, u32[256]{0:T(256)}, u32[]{:S(2)}) copy-start(u32[256]{0:T(256)} %constant.53) | copy-start | bytes 3076
  32.0 15.3 %copy-start.2 = (s32[1,32]{1,0:T(1,128)S(1)}, s32[1,32]{1,0:T(1,128)}, u32[]{:S(2)}) copy-start(s32[1,32]{1,0:T(1,128)} %param.12) | copy-start | bytes 388
  32.0 123.1 %all-to-all-start = ((bf16[32,32,4096]{2,1,0:T(8,128)(2,1)}), bf16[32,32,4096]{2,1,0:T(8,128)(2,1)}, u32[]{:S(2)}, u32[]{:S(2)}) async-start(bf16[32,32,4096]{2,1,0:T(8,128)(2,1)} %stack.2), calls=%async_computation | async-start | bytes 16777216 | tf_op jit(solution)/shard_map/all_to_all | solution.py:26
  163.4 150.5 %copy-start.1 = (s32[1,32]{1,0:T(1,128)S(1)}, s32[1,32]{1,0:T(1,128)}, u32[]{:S(2)}) copy-start(s32[1,32]{1,0:T(1,128)} %param.13) | copy-start | bytes 388

commit v2 on v0

--- a/solution.py
+++ b/solution.py
@@ -36,7 +36,7 @@
     top = lax.pmax(stats[0], ("dp", "tensor"))
     factor = jnp.exp(stats[0] - top)
     total, weighted, chosen = lax.psum(
-        (stats[1] * factor, stats[2] * factor, stats[3]), ("dp", "tensor")
+        lax.psum((stats[1] * factor, stats[2] * factor, stats[3]), "dp"), "tensor"
     )
     lse = top + jnp.log(total)
     score = chosen - lse

time: 266 us -> 343 us (1.29)
  the two profiles are of different devices: /device:TPU:1 before, /device:TPU:0 now
where the time goes in v2:
time: 343 us
  blocking collectives  274 us (80%)
  waiting for transfers between devices  37.7 us (11%)
  between operations  15.5 us (5%)
  matrix products  8.27 us (2%)
  other arithmetic  4.44 us (1%)
    psum x1, blocking collectives, per_device(): lax.psum((stats[1] * factor, stats[2] * factor, stats[3]), 'dp')  125 us
    pmax x1, blocking collectives, per_device(): top = lax.pmax(stats[0], ('dp', 'tensor'))  76.2 us
    all_gather x1, waiting for transfers between devices, per_device(): rows_piece = lax.all_gather(normed, 'dp', axis=0, tiled=True)  37.6 us
    psum x1, blocking collectives, per_device(): lax.psum(lax.psum((stats[1] * factor, stats[2] * factor, stats[3]), 'dp')...  28.9 us
    all_gather x1, blocking collectives, per_device(): full_rows = lax.all_gather(picked, 'tensor', axis=1, tiled=True)  26.8 us
    unnamed x1, blocking collectives  16.9 us
    dot_general x1, matrix products, per_device(): logits = jnp.dot(rows_piece, head, preferred_element_type=jnp.float32)  8.27 us
  transfers between devices with their start and end apart: 1, of which 1 were waited for; matrix products, arithmetic and copies ran while one was open for 1% of the time, Pallas kernels for 0%

profile of v2, /device:TPU:0, one launch (start us, length us, event | category | flops | bytes accessed | tf_op | source)
XLA Modules:
  0.0 342.6 jit_solution(2010032841744142775)
XLA Ops:
  7.2 0.0 copy-start
  7.2 0.0 all-gather.3.cloned.1.call-start
  7.9 0.7 fusion.7
  8.6 0.7 compare_and_fusion
  9.3 0.0 copy-done
  9.3 0.6 gather_fusion
  9.9 0.1 broadcast_select_fusion
  10.0 26.8 %all_gather.10 = bf16[32,4096]{1,0:T(8,128)(2,1)S(1)} all-gather(bf16[32,512]{1,0:T(8,128)(2,1)S(1)} %broadcast_select_fusion), channel_id=1, replica_groups=mesh['dp'=32,'tensor'=8] {'tensor'}, dimensions={1}, use_global_device_ids=true | all-gather | bytes 294912 | tf_op jit(solution)/shard_map/all_gather | solution.py:13
  36.8 0.2 fusion.1
  37.0 1.6 fusion.3
  38.6 0.0 all-gather.3.cloned.1.call-update
  38.6 1.3 dynamic-slice
  40.5 0.8 bitcast_dynamic-update-slice_fusion
  41.3 16.9 %all-reduce = s32[1024]{0:T(1024)S(1)} all-reduce(s32[1024]{0:T(1024)S(1)} %bitcast_dynamic-update-slice_fusion), channel_id=2, replica_groups=mesh['dp'=32,'tensor'=8] {'dp'}, use_global_device_ids=true, to_apply=%add | all-reduce | flops 1024 | bytes 8192
  58.2 37.6 %all-gather.3.cloned.1.call-done = bf16[1024,4096]{1,0:T(8,128)(2,1)} async-done(((bf16[32,4096]{1,0:T(8,128)(2,1)}), bf16[1024,4096]{1,0:T(8,128)(2,1)}) %all-gather.3.cloned.1.call-update) | async-done | bytes 8388624 | tf_op jit(solution)/shard_map/all_gather | solution.py:25
  95.8 8.3 %fusion.10 = (f32[1024]{0:T(1024)S(1)}, f32[1024,512]{0,1:T(8,128)S(1)}) fusion(bf16[1024,4096]{1,0:T(8,128)(2,1)} %all-gather.3.cloned.1.call-done, bf16[4096,512]{1,0:T(8,128)(2,1)} %param.9), kind=kOutput, calls=%fused_computation.30 | convolution fusion | flops 4295490560 | bytes 14684160 | tf_op jit(solution)/shard_map/dot_general | solution.py:27
  104.1 0.0 copy-start.1
  104.1 76.2 %pmax.7 = f32[1024]{0:T(1024)S(1)} all-reduce(f32[1024]{0:T(1024)S(1)} %get-tuple-element.17), channel_id=1, replica_groups=mesh['dp'=32,'tensor'=8] {'dp','tensor'}, use_global_device_ids=true, to_apply=%region_5.6 | all-reduce | flops 1024 | bytes 8192 | tf_op jit(solution)/shard_map/pmax | solution.py:36
  180.3 0.7 multiply_reduce_fusion
  181.0 125.2 %all-reduce.1 = (f32[1024]{0:T(1024)S(1)}, f32[1024]{0:T(1024)S(1)}, f32[1024]{0:T(1024)S(1)}) all-reduce(f32[1024]{0:T(1024)S(1)} %get-tuple-element.4, f32[1024]{0:T(1024)S(1)} %get-tuple-element.14, f32[1024]{0:T(1024)S(1)} %get-tuple-element.13), channel_id=1, replica_groups=mesh['dp'=32,'tensor'=8] {'dp'}, use_global_device_ids=true, to_apply=%region_2.3 | all-reduce | flops 3072 | bytes 24576 | tf_op jit(solution)/shard_map/psum | solution.py:39
  306.2 28.9 %all-reduce.2 = (f32[1024]{0:T(1024)S(1)}, f32[1024]{0:T(1024)S(1)}, f32[1024]{0:T(1024)S(1)}) all-reduce(f32[1024]{0:T(1024)S(1)} %get-tuple-element.5, f32[1024]{0:T(1024)S(1)} %get-tuple-element.6, f32[1024]{0:T(1024)S(1)} %get-tuple-element.7), channel_id=1, replica_groups=mesh['dp'=32,'tensor'=8] {'tensor'}, use_global_device_ids=true, to_apply=%region_3.4 | all-reduce | flops 3072 | bytes 24576 | tf_op jit(solution)/shard_map/psum | solution.py:38
  335.2 0.0 copy-done.1
  335.2 0.6 fusion.9
  (6 shorter events, 0.0 us)
Async XLA Ops:
  7.2 2.1 copy-start
  7.2 88.7 %all-gather.3.cloned.1.call-start = ((), (), s32[]{:S(2)}) async-start(), calls=%async_computation | async-start | bytes 8650752 | tf_op jit(solution)/shard_map/all_gather | solution.py:25
  104.1 231.0 %copy-start.1 = (s32[1,32]{1,0:T(1,128)S(1)}, s32[1,32]{1,0:T(1,128)}, u32[]{:S(2)}) copy-start(s32[1,32]{1,0:T(1,128)} %param.13) | copy-start | bytes 388
Sparse Core Ops, SparseCore 0:
  38.7 57.0 all-gather.2
